TPU v7x, 32 devices: a whole 2x2x4 slice. The times are simulated.
32 devices in a mesh: parts: 2 (over y), dp: 4 (over z), tensor: 2 (over x), group: 2 (over core).
Axes of the slice: x: 2, y: 2, z: 4, core: 2. Of those that a mesh axis runs over, the one named last changes fastest.
Arguments:
- activations: bfloat16 [1, 32, 256, 4096], P(None, ('parts', 'dp'), None, ('tensor', 'group')), parts along dimension 1, may hold values from -6 to 6
- out_grads: bfloat16 [1, 32, 256, 14336], P(None, ('parts', 'dp'), None, ('tensor', 'group')), parts along dimension 1, may hold values from -6 to 6
- proj_in: bfloat16 [1, 4096, 64], P(None, ('tensor', 'group')), may hold values from -0.09375 to 0.09375
- proj_out: bfloat16 [1, 14336, 64], P(None, ('tensor', 'group')), may hold values from -0.046875 to 0.046875
- queries: bfloat16 [4096, 4096], P(('parts', 'tensor', 'group'), 'dp'), parts along dimension 0, may hold values from -0.005859375 to 0.005859375
Outputs:
- scores: float32 [16, 4096], P('dp', ('parts', 'tensor', 'group')), parts along dimension 1
There are 2 independent parts, one for each index of `parts`. A program takes and returns all parts, laid end to end along the dimension named above; an argument that names none is the same for every part. Nothing has to cross between parts.
All inputs are finite; a program needn't handle non-finite values.
Results may differ from a plain program's by a relative error of at most 0.005.
Values may be sent and summed in bfloat16 or wider, within the bound.
A program may use at most 64 MiB of HBM per device.

v0:
```python
import jax
import jax.numpy as jnp
from jax import lax
from jax.sharding import PartitionSpec as P


def shards(activations, out_grads, proj_in, proj_out, queries):
    proj_acts = jnp.einsum(
        "lsth,lhr->lstr", activations, proj_in, preferred_element_type=jnp.float32
    )
    proj_grads = jnp.einsum(
        "lsth,lhr->lstr", out_grads, proj_out, preferred_element_type=jnp.float32
    )
    summed_acts, summed_grads = lax.psum((proj_acts, proj_grads), ("tensor", "group"))
    outer = jnp.einsum(
        "lsta,lstb->slab",
        summed_grads.astype(jnp.bfloat16),
        summed_acts.astype(jnp.bfloat16),
        preferred_element_type=jnp.float32,
    )
    seq_count = outer.shape[0]
    example_grads = outer.reshape(seq_count, -1).astype(jnp.bfloat16)
    traded = lax.all_to_all(example_grads, "dp", split_axis=1, concat_axis=0, tiled=True)
    return lax.psum_scatter(
        lax.dot_general(
            traded, queries, (((1,), (1,)), ((), ())), preferred_element_type=jnp.float32
        ),
        "dp",
        scatter_dimension=0,
        tiled=True,
    )


def solution(mesh):
    placed = (
        P(None, ("parts", "dp"), None, ("tensor", "group")),
        P(None, ("parts", "dp"), None, ("tensor", "group")),
        P(None, ("tensor", "group"), None),
        P(None, ("tensor", "group"), None),
        P(("parts", "tensor", "group"), "dp"),
    )
    return jax.shard_map(
        shards,
        mesh=mesh,
        in_specs=placed,
        out_specs=P("dp", ("parts", "tensor", "group")),
        check_vma=False,
    )
```

profile of v0, /device:TPU:0, one launch (start us, length us, event | category | flops | bytes accessed | tf_op | source)
XLA Modules:
  0.0 57.4 jit_solution(16096773874334835234)
XLA Ops:
  0.0 0.0 copy-start
  0.0 0.0 copy-start.1
  0.0 1.6 %copy-done = bf16[1,4,256,1024]{3,2,1,0:T(8,128)(2,1)S(1)} copy-done((bf16[1,4,256,1024]{3,2,1,0:T(8,128)(2,1)S(1)}, bf16[1,4,256,1024]{3,2,1,0:T(8,128)(2,1)}, u32[]{:S(2)}) %copy-start) | copy-done | bytes 2097176
  1.6 1.7 %fusion.4 = f32[1,4,256,64]{2,3,1,0:T(8,128)S(1)} fusion(bf16[1,4,256,1024]{3,2,1,0:T(8,128)(2,1)S(1)} %copy-done, bf16[1,1024,64]{1,2,0:T(8,128)(2,1)} %param.7), kind=kOutput, calls=%fused_computation.4 | convolution fusion | flops 134217728 | bytes 2490368 | tf_op jit(solution)/shard_map/lsth,lhr->lstr/dot_general | solution.py:8
  3.3 5.5 %fusion.7 = f32[1,4,256,64]{2,3,1,0:T(8,128)S(1)} fusion(bf16[1,4,256,3584]{3,2,1,0:T(8,128)(2,1)} %param.6, bf16[1,3584,64]{1,2,0:T(8,128)(2,1)} %param.8), kind=kOutput, calls=%fused_computation.5 | convolution fusion | flops 469762048 | bytes 8060928 | tf_op jit(solution)/shard_map/lsth,lhr->lstr/dot_general | solution.py:11
  8.7 18.7 %all-reduce.3 = (bf16[1,4,256,64]{2,3,1,0:T(8,128)(2,1)S(1)}, bf16[1,4,256,64]{2,3,1,0:T(8,128)(2,1)S(1)}) all-reduce(f32[1,4,256,64]{2,3,1,0:T(8,128)S(1)} %fusion.4, f32[1,4,256,64]{2,3,1,0:T(8,128)S(1)} %fusion.7), channel_id=1, replica_groups=mesh['parts'=2,'dp'=4,'tensor'=2,'group'=2] {'tensor','group'}, use_global_device_ids=true, to_apply=%region_1.0 | all-reduce | flops 131072 | bytes 786432 | tf_op jit(solution)/shard_map/psum | solution.py:14
  27.4 0.2 convolution_convert_fusion
  27.6 0.1 convert_element_type.16
  27.7 0.6 %copy.7 = bf16[4,4,1024]{2,0,1:T(4,128)(2,1)} copy(bf16[4,4,1024]{2,1,0:T(4,128)(2,1)S(1)} %convert_element_type.16) | data formatting | bytes 65536 | tf_op jit(solution)/shard_map/convert_element_type | solution.py:22
  28.3 4.9 %all-to-all-start = ((bf16[4,4,1024]{2,0,1:T(4,128)(2,1)}), bf16[4,4,1024]{2,0,1:T(4,128)(2,1)S(1)}, u32[]{:S(2)}, u32[]{:S(2)}) async-start(bf16[4,4,1024]{2,0,1:T(4,128)(2,1)} %copy.7), calls=%async_computation | async-start | bytes 65536 | tf_op jit(solution)/shard_map/all_to_all | solution.py:23
  33.1 0.0 copy-done.1
  33.1 0.6 %dynamic-slice = u32[1]{0:T(128)} dynamic-slice(u32[32]{0:T(128)S(1)} %copy-done.1, u32[]{:T(128)S(6)} %add.7), dynamic_slice_sizes={1} | dynamic-slice | bytes 12
  34.4 4.4 %all-to-all-done = bf16[4,4,1024]{2,0,1:T(4,128)(2,1)S(1)} async-done(((bf16[4,4,1024]{2,0,1:T(4,128)(2,1)}), bf16[4,4,1024]{2,0,1:T(4,128)(2,1)S(1)}, u32[]{:S(2)}, u32[]{:S(2)}) %all-to-all-start) | async-done | bytes 32800 | tf_op jit(solution)/shard_map/all_to_all | solution.py:23
  38.8 1.6 %fusion.16 = f32[16,512]{1,0:T(8,128)S(1)} fusion(bf16[16,1024]{1,0:T(8,128)(2,1)S(1)} %all_to_all.14, bf16[512,1024]{1,0:T(8,128)(2,1)} %param.9), kind=kOutput, calls=%fused_computation.14 | convolution fusion | flops 16777216 | bytes 1114112 | tf_op jit(solution)/shard_map/dot_general | solution.py:25
  40.4 16.4 %all-reduce = f32[16,512]{1,0:T(8,128)S(1)} all-reduce(f32[16,512]{1,0:T(8,128)S(1)} %fusion.16), channel_id=2, replica_groups=mesh['parts'=2,'dp'=4,'tensor'=2,'group'=2] {'dp'}, use_global_device_ids=true, to_apply=%region_2.0.clone | all-reduce | flops 8192 | bytes 65536
  56.8 0.6 %constant_dynamic-slice_fusion = f32[4,512]{1,0:T(4,128)} fusion(f32[16,512]{1,0:T(8,128)S(1)} %all-reduce, u32[]{:T(128)S(6)} %multiply.1), kind=kLoop, calls=%fused_computation.13 | loop fusion | bytes 16388
  (1 shorter events, 0.0 us)
Async XLA Ops:
  0.0 1.6 %copy-start = (bf16[1,4,256,1024]{3,2,1,0:T(8,128)(2,1)S(1)}, bf16[1,4,256,1024]{3,2,1,0:T(8,128)(2,1)}, u32[]{:S(2)}) copy-start(bf16[1,4,256,1024]{3,2,1,0:T(8,128)(2,1)} %param.5) | copy-start | bytes 6291460
  0.0 33.1 %copy-start.1 = (u32[32]{0:T(128)S(1)}, u32[32]{0:T(128)}, u32[]{:S(2)}) copy-start(u32[32]{0:T(128)} %constant.4) | copy-start | bytes 388
  28.3 10.5 %all-to-all-start = ((bf16[4,4,1024]{2,0,1:T(4,128)(2,1)}), bf16[4,4,1024]{2,0,1:T(4,128)(2,1)S(1)}, u32[]{:S(2)}, u32[]{:S(2)}) async-start(bf16[4,4,1024]{2,0,1:T(4,128)(2,1)} %copy.7), calls=%async_computation | async-start | bytes 65536 | tf_op jit(solution)/shard_map/all_to_all | solution.py:23
where the time goes:
time: 57.8 us; the launch traced here: 57.4 us
  blocking collectives  35.1 us (61%)
  matrix products  8.89 us (15%)
  starting transfers between devices  4.86 us (8%)
  waiting for transfers between devices  4.42 us (8%)
  local copies, waits for them, and re-layouts  3.53 us (6%)
  between operations  0.69 us (1%)
    psum x1, blocking collectives, shards(): lax.psum((proj_acts, proj_grads), ('tensor', 'group'))  18.7 us
    unnamed x1, blocking collectives  16.4 us
    dot_general x1, matrix products, shards(): jnp.einsum('lsth,lhr->lstr', out_grads, proj_out, preferred_element_type=...  5.46 us
    all_to_all x1, starting transfers between devices, shards(): lax.all_to_all(example_grads, 'dp', split_axis=1, concat_axis=0, tiled=True)  4.86 us
    all_to_all x1, waiting for transfers between devices, shards(): lax.all_to_all(example_grads, 'dp', split_axis=1, concat_axis=0, tiled=True)  4.42 us
    unnamed x6, local copies, waits for them, and re-layouts  2.78 us
    dot_general x1, matrix products, shards(): jnp.einsum('lsth,lhr->lstr', activations, proj_in, preferred_element_type...  1.66 us
    dot_general x1, matrix products, shards(): lax.dot_general(traded, queries, (((1,), (1,)), ((), ())), preferred_elem...  1.6 us
  transfers between devices with their start and end apart: 1, of which 1 were waited for; matrix products, arithmetic and copies ran while one was open for 1% of the time, Pallas kernels for 0%

commit v1 on v0

--- a/solution.py
+++ b/solution.py
@@ -11,7 +11,7 @@
     proj_grads = jnp.einsum(
         "lsth,lhr->lstr", out_grads, proj_out, preferred_element_type=jnp.float32
     )
-    summed_acts, summed_grads = lax.psum((proj_acts, proj_grads), ("tensor", "group"))
+    summed_acts, summed_grads = lax.psum(lax.psum((proj_acts, proj_grads), "group"), "tensor")
     outer = jnp.einsum(
         "lsta,lstb->slab",
         summed_grads.astype(jnp.bfloat16),

time: 57.8 us -> 93 us (1.61)
  waiting for transfers between devices: 4.42 us -> 26 us
  between operations: 0.69 us -> 14.1 us
    psum x0 -> x1, waiting for transfers between devices: none -> 21.5 us  [shards(): lax.psum((proj_acts, proj_grads), 'group')]
    dot_general x1, matrix products: 1.6 us -> 0.37 us  [shards(): lax.dot_general(traded, queries, (((1,), (1,)), ((), ())), preferred_elem...]
    unnamed x6 -> x8, local copies, waits for them, and re-layouts: 2.78 us -> 2.78 us
  transfers between devices with their start and end apart: 1 -> 2, of which waited for: 1 -> 2; matrix products, arithmetic and copies ran while one was open for 1% -> 1% of each run, Pallas kernels for 0% -> 0%
where the time goes in v1:
time: 93 us; the launch traced here: 92.7 us
  blocking collectives  35.4 us (38%)
  waiting for transfers between devices  26 us (28%)
  between operations  14.1 us (15%)
  matrix products  9.07 us (10%)
  starting transfers between devices  4.6 us (5%)
  local copies, waits for them, and re-layouts  3.53 us (4%)
    psum x1, waiting for transfers between devices, shards(): lax.psum((proj_acts, proj_grads), 'group')  21.5 us
    psum x1, blocking collectives, shards(): lax.psum(lax.psum((proj_acts, proj_grads), 'group'), 'tensor')  19 us
    unnamed x1, blocking collectives  16.4 us
    dot_general x1, matrix products, shards(): jnp.einsum('lsth,lhr->lstr', out_grads, proj_out, preferred_element_type=...  6.17 us
    all_to_all x1, starting transfers between devices, shards(): lax.all_to_all(example_grads, 'dp', split_axis=1, concat_axis=0, tiled=True)  4.6 us
    all_to_all x1, waiting for transfers between devices, shards(): lax.all_to_all(example_grads, 'dp', split_axis=1, concat_axis=0, tiled=True)  4.42 us
    unnamed x8, local copies, waits for them, and re-layouts  2.78 us
    dot_general x1, matrix products, shards(): jnp.einsum('lsth,lhr->lstr', activations, proj_in, preferred_element_type...  2.36 us
  transfers between devices with their start and end apart: 2, of which 2 were waited for; matrix products, arithmetic and copies ran while one was open for 1% of the time, Pallas kernels for 0%

profile of v1, /device:TPU:0, one launch (start us, length us, event | category | flops | bytes accessed | tf_op | source)
XLA Modules:
  0.0 92.7 jit_solution(9786813681891488460)
XLA Ops:
  6.5 0.0 copy-start
  6.5 0.0 copy-start.2
  6.5 0.0 copy-start.1
  6.5 0.0 all-reduce.6.cloned.1.call-start
  6.5 1.6 %copy-done = bf16[1,4,256,1024]{3,2,1,0:T(8,128)(2,1)S(1)} copy-done((bf16[1,4,256,1024]{3,2,1,0:T(8,128)(2,1)S(1)}, bf16[1,4,256,1024]{3,2,1,0:T(8,128)(2,1)}, u32[]{:S(2)}) %copy-start) | copy-done | bytes 2097176
  8.1 2.4 %fusion.4 = f32[1,4,256,64]{2,3,1,0:T(8,128)} fusion(bf16[1,4,256,1024]{3,2,1,0:T(8,128)(2,1)S(1)} %copy-done, bf16[1,1024,64]{1,2,0:T(8,128)(2,1)} %param.7), kind=kOutput, calls=%fused_computation.4 | convolution fusion | flops 134217728 | bytes 2490368 | tf_op jit(solution)/shard_map/lsth,lhr->lstr/dot_general | solution.py:8
  10.5 6.2 %fusion.7 = f32[1,4,256,64]{2,3,1,0:T(8,128)} fusion(bf16[1,4,256,3584]{3,2,1,0:T(8,128)(2,1)} %param.6, bf16[1,3584,64]{1,2,0:T(8,128)(2,1)} %param.8), kind=kOutput, calls=%fused_computation.5 | convolution fusion | flops 469762048 | bytes 8060928 | tf_op jit(solution)/shard_map/lsth,lhr->lstr/dot_general | solution.py:11
  16.7 0.0 all-reduce.6.cloned.1.call-update
  16.7 21.5 %all-reduce.6.cloned.1.call-done = (f32[1,4,256,64]{2,3,1,0:T(8,128)}, f32[1,4,256,64]{2,3,1,0:T(8,128)}) async-done(((f32[1,4,256,64]{2,3,1,0:T(8,128)}, f32[1,4,256,64]{2,3,1,0:T(8,128)}), (f32[1,4,256,64]{2,3,1,0:T(8,128)}, f32[1,4,256,64]{2,3,1,0:T(8,128)})) %all-reduce.6.cloned.1.call-update) | async-done | bytes 524304 | tf_op jit(solution)/shard_map/psum | solution.py:14
  38.2 19.0 %all-reduce.7 = (bf16[1,4,256,64]{2,3,1,0:T(8,128)(2,1)S(1)}, bf16[1,4,256,64]{2,3,1,0:T(8,128)(2,1)S(1)}) all-reduce(f32[1,4,256,64]{2,3,1,0:T(8,128)} %get-tuple-element.5, f32[1,4,256,64]{2,3,1,0:T(8,128)} %get-tuple-element.6), channel_id=1, replica_groups=mesh['parts'=2,'dp'=4,'tensor'=2,'group'=2] {'tensor'}, use_global_device_ids=true, to_apply=%region_3.0 | all-reduce | flops 131072 | bytes 786432 | tf_op jit(solution)/shard_map/psum | solution.py:14
  57.2 0.2 convolution_convert_fusion
  57.4 0.1 convert_element_type.16
  57.5 0.6 copy.7
  58.2 4.6 %all-to-all-start = ((bf16[4,4,1024]{2,0,1:T(4,128)(2,1)}), bf16[4,4,1024]{2,0,1:T(4,128)(2,1)S(1)}, u32[]{:S(2)}, u32[]{:S(2)}) async-start(bf16[4,4,1024]{2,0,1:T(4,128)(2,1)} %copy.7), calls=%async_computation | async-start | bytes 65536 | tf_op jit(solution)/shard_map/all_to_all | solution.py:23
  62.8 0.0 copy-done.2
  62.8 0.6 dynamic-slice
  64.0 4.4 %all-to-all-done = bf16[4,4,1024]{2,0,1:T(4,128)(2,1)S(1)} async-done(((bf16[4,4,1024]{2,0,1:T(4,128)(2,1)}), bf16[4,4,1024]{2,0,1:T(4,128)(2,1)S(1)}, u32[]{:S(2)}, u32[]{:S(2)}) %all-to-all-start) | async-done | bytes 32800 | tf_op jit(solution)/shard_map/all_to_all | solution.py:23
  68.4 0.0 copy-done.1
  68.4 0.4 fusion.16
  68.8 16.4 %all-reduce = f32[16,512]{1,0:T(8,128)S(1)} all-reduce(f32[16,512]{1,0:T(8,128)S(1)} %fusion.16), channel_id=2, replica_groups=mesh['parts'=2,'dp'=4,'tensor'=2,'group'=2] {'dp'}, use_global_device_ids=true, to_apply=%region_4.0.clone | all-reduce | flops 8192 | bytes 65536
  85.2 0.6 constant_dynamic-slice_fusion
  (1 shorter events, 0.0 us)
Async XLA Ops:
  6.5 1.6 %copy-start = (bf16[1,4,256,1024]{3,2,1,0:T(8,128)(2,1)S(1)}, bf16[1,4,256,1024]{3,2,1,0:T(8,128)(2,1)}, u32[]{:S(2)}) copy-start(bf16[1,4,256,1024]{3,2,1,0:T(8,128)(2,1)} %param.5) | copy-start | bytes 6291460
  6.5 56.2 %copy-start.2 = (u32[32]{0:T(128)S(1)}, u32[32]{0:T(128)}, u32[]{:S(2)}) copy-start(u32[32]{0:T(128)} %constant.4) | copy-start | bytes 388
  6.5 61.9 %copy-start.1 = (bf16[512,1024]{1,0:T(8,128)(2,1)S(1)}, bf16[512,1024]{1,0:T(8,128)(2,1)}, u32[]{:S(2)}) copy-start(bf16[512,1024]{1,0:T(8,128)(2,1)} %param.9) | copy-start | bytes 3145732
  6.5 31.7 %all-reduce.6.cloned.1.call-start = ((), (), s32[]{:S(2)}) async-start(), calls=%async_computation.1 | async-start | bytes 1048576 | tf_op jit(solution)/shard_map/psum | solution.py:14
  58.2 10.3 %all-to-all-start = ((bf16[4,4,1024]{2,0,1:T(4,128)(2,1)}), bf16[4,4,1024]{2,0,1:T(4,128)(2,1)S(1)}, u32[]{:S(2)}, u32[]{:S(2)}) async-start(bf16[4,4,1024]{2,0,1:T(4,128)(2,1)} %copy.7), calls=%async_computation | async-start | bytes 65536 | tf_op jit(solution)/shard_map/all_to_all | solution.py:23
Sparse Core Ops, SparseCore 0:
  16.8 21.3 all-reduce.5
